TPU v7x, 32 devices: a whole 2x2x4 slice. The times are simulated.
32 devices in a mesh: grp: 2 (over x), seq: 16 (over z, y, core).
Axes of the slice: x: 2, y: 2, z: 4, core: 2. Of those that a mesh axis runs over, the one named last changes fastest.
Arguments:
- image_qkv: bfloat16 [3, 8, 16, 896, 128], P(None, 'grp', None, 'seq'), parts along dimension 1, may hold values from -16 to 16
- text_kv: bfloat16 [2, 2, 8, 16, 512, 128], P(None, None, 'grp', None, 'seq'), parts along dimension 2, may hold values from -6 to 6
- prompt_ids: int32 [2, 8, 512], P(None, 'grp'), parts along dimension 1, may hold values from 0 to 32127, as said below
- timesteps: int32 [8], P('grp'), parts along dimension 0, may hold values from 0 to 999
- image_states: bfloat16 [8, 896, 1536], P('grp', 'seq'), parts along dimension 0, may hold values from -6 to 6
- frozen_out: bfloat16 [2048, 1536], P('seq'), may hold values from -0.125 to 0.125
- trainee_out: bfloat16 [4096, 1536], P(('grp', 'seq')), parts along dimension 0, may hold values from -0.125 to 0.125
- time_mod: bfloat16 [256, 3072], replicated, may hold values from -0.375 to 0.375
- final_head: bfloat16 [1536, 64], replicated, may hold values from -0.15625 to 0.15625
Outputs:
- weight_grad: float32 [4096, 1536], P(('grp', 'seq')), parts along dimension 0
There are 2 independent parts, one for each index of `grp`. A program takes and returns all parts, laid end to end along the dimension named above; an argument that names none is the same for every part. Nothing has to cross between parts.
Inputs may be any that keep to these rules, and one draw needn't show every extreme that they name: `prompt_ids`: zero marks padding; in each row of 512 ids the padding is a suffix and position 0 is never padding.
All inputs are finite; a program needn't handle non-finite values.
Results may differ from a plain program's by a relative error of at most 0.011.
Values may be sent and summed in bfloat16 or wider, within the bound.
No kernel may reach another device: no remote copies, remote signals or barrier semaphores. Data moves between devices by JAX's collectives and lax.ppermute only.
A program may use at most 128 MiB of HBM per device.

v0:
```python
import math
import jax
import jax.numpy as jnp
from jax import lax
from jax.sharding import PartitionSpec as P

SAMPLES = 4
HEADS = 16
HEAD_DIM = 128
WIDTH = 1536
TIME_DIM = 256


def image_block(queries, image_keys, image_values):
    factor = HEAD_DIM ** (-0.5)
    image_scores = jnp.dot(queries, image_keys.T, preferred_element_type=jnp.float32) * factor
    image_max = jnp.max(image_scores, axis=1, keepdims=True)
    image_exp = jnp.exp(image_scores - image_max)
    image_total = jnp.sum(image_exp, axis=1, keepdims=True)
    image_part = jnp.dot(
        image_exp.astype(jnp.bfloat16), image_values, preferred_element_type=jnp.float32
    )
    return (image_max, image_total, image_part)


def text_finish(queries, image_stats, text_keys, text_values, allowed_text):
    factor = HEAD_DIM ** (-0.5)
    image_max, image_total, image_part = image_stats
    text_scores = jnp.dot(queries, text_keys.T, preferred_element_type=jnp.float32) * factor
    text_scores = jnp.where(allowed_text[None, :], text_scores, -jnp.inf)
    pass_max = jnp.maximum(image_max, jnp.max(text_scores, axis=1, keepdims=True))
    ratio = jnp.exp(image_max - pass_max)
    text_exp = jnp.exp(text_scores - pass_max)
    text_part = jnp.dot(
        text_exp.astype(jnp.bfloat16), text_values, preferred_element_type=jnp.float32
    )
    numer = ratio * image_part + text_part
    denom = ratio * image_total + jnp.sum(text_exp, axis=1, keepdims=True)
    return (numer / denom).astype(jnp.bfloat16)


def head_out(branch, states, gate, scale, final_head):
    mixed = states.astype(jnp.float32) + gate[:, None, :] * branch
    normed = (
        mixed
        * lax.rsqrt(jnp.mean(mixed * mixed, axis=-1, keepdims=True) + 1e-06)
        * (1.0 + scale[:, None, :])
    )
    normed = normed.astype(jnp.bfloat16)
    return jnp.einsum("bic,cd->bid", normed, final_head, preferred_element_type=jnp.float32)


def shards(
    image_qkv,
    text_kv,
    prompt_ids,
    timesteps,
    image_states,
    frozen_out,
    trainee_out,
    time_mod,
    final_head,
):
    group_size = lax.axis_size("seq")
    position = lax.axis_index("seq")
    image_dev = image_qkv.shape[3]
    text_dev = text_kv.shape[4]
    item_count = SAMPLES * HEADS
    owned_count = item_count // group_size
    token_rows = SAMPLES * image_dev
    image_all = image_dev * group_size
    block_rows = image_dev * min(group_size, 8)
    block_count = image_all // block_rows
    image_local = image_qkv.transpose(0, 2, 1, 3, 4).reshape(3, item_count, image_dev, HEAD_DIM)
    text_local = text_kv.transpose(0, 1, 3, 2, 4, 5).reshape(4, item_count, text_dev, HEAD_DIM)
    image_heads, text_heads = (
        lax.all_to_all(image_local, "seq", split_axis=1, concat_axis=2, tiled=True),
        lax.all_to_all(text_local, "seq", split_axis=1, concat_axis=2, tiled=True),
    )
    owned_items = position * owned_count + jnp.arange(owned_count, dtype=jnp.int32)
    sample_of = owned_items % SAMPLES
    selector = (sample_of[:, None] == jnp.arange(SAMPLES, dtype=jnp.int32)[None, :]).astype(
        jnp.float32
    )
    live_all = (prompt_ids != 0).astype(jnp.float32)
    live_owned = jnp.einsum("jb,pbt->pjt", selector, live_all) > 0.5

    def query_blocks(item_index):
        return image_heads[0, item_index].reshape(block_count, block_rows, HEAD_DIM)

    def joint_item(item_index):
        image_keys = image_heads[1, item_index]
        image_values = image_heads[2, item_index]

        def per_block(queries):
            stats = image_block(queries, image_keys, image_values)
            concept = text_finish(
                queries,
                stats,
                text_heads[0, item_index],
                text_heads[1, item_index],
                live_owned[0, item_index],
            )
            null = text_finish(
                queries,
                stats,
                text_heads[2, item_index],
                text_heads[3, item_index],
                live_owned[1, item_index],
            )
            return jnp.stack([concept, null])

        blocks = lax.map(per_block, query_blocks(item_index))
        return blocks.transpose(1, 0, 2, 3).reshape(2, image_all, HEAD_DIM)

    both_passes = lax.map(joint_item, jnp.arange(owned_count, dtype=jnp.int32)).transpose(
        1, 0, 2, 3
    )
    returned = lax.all_to_all(both_passes, "seq", split_axis=2, concat_axis=1, tiled=True)
    attention = returned.reshape(2, HEADS, SAMPLES, image_dev, HEAD_DIM).transpose(0, 2, 3, 1, 4)
    attention = attention.reshape(2, token_rows, HEADS * HEAD_DIM)
    half_dim = TIME_DIM // 2
    freqs = jnp.exp(-math.log(10000.0) * jnp.arange(half_dim, dtype=jnp.float32) / half_dim)
    angles = timesteps.astype(jnp.float32)[:, None] * freqs[None, :]
    embedding = jnp.concatenate([jnp.cos(angles), jnp.sin(angles)], 1)
    modulation = jnp.dot(embedding, time_mod.astype(jnp.float32), precision=lax.Precision.HIGHEST)
    gate = modulation[:, :WIDTH]
    scale = modulation[:, WIDTH:]
    piece_frozen = lax.all_gather(frozen_out, "seq", axis=0, tiled=True)
    piece_trainee = lax.all_gather(trainee_out, "seq", axis=0, tiled=True)
    columns_c = attention[0]
    columns_n = attention[1]
    branch_c = jnp.dot(columns_c, piece_frozen, preferred_element_type=jnp.float32)
    branch_n = jnp.dot(columns_n, piece_frozen, preferred_element_type=jnp.float32)
    branch_s = jnp.dot(columns_c, piece_trainee, preferred_element_type=jnp.float32)
    branch_c = branch_c.reshape(SAMPLES, image_dev, WIDTH)
    branch_n = branch_n.reshape(SAMPLES, image_dev, WIDTH)
    branch_s = branch_s.reshape(SAMPLES, image_dev, WIDTH)
    velocity_c = head_out(branch_c, image_states, gate, scale, final_head)
    velocity_n = head_out(branch_n, image_states, gate, scale, final_head)
    target = velocity_n - (velocity_c - velocity_n)

    def student(branch):
        velocity_s = head_out(branch, image_states, gate, scale, final_head)
        return jnp.sum((velocity_s - target) ** 2) / SAMPLES

    loss_part, pull = jax.vjp(student, branch_s)
    (cotangent,) = pull(jnp.ones_like(loss_part))
    cotangent_samples = cotangent.astype(jnp.bfloat16)
    cotangent_rows = cotangent_samples.reshape(token_rows, WIDTH)
    columns = attention[0]
    return lax.psum_scatter(
        lax.dot_general(
            columns, cotangent_rows, (((0,), (0,)), ((), ())), preferred_element_type=jnp.float32
        ),
        "seq",
        scatter_dimension=0,
        tiled=True,
    )


def solution(mesh):
    return jax.shard_map(
        shards,
        mesh=mesh,
        in_specs=(
            P(None, "grp", None, "seq", None),
            P(None, None, "grp", None, "seq", None),
            P(None, "grp", None),
            P("grp"),
            P("grp", "seq", None),
            P("seq", None),
            P(("grp", "seq"), None),
            P(),
            P(),
        ),
        out_specs=P(("grp", "seq"), None),
        check_vma=False,
    )
```

profile of v0, /device:TPU:0, one launch (start us, length us, event | category | flops | bytes accessed | tf_op | source)
XLA Modules:
  0.0 544.9 jit_solution(13315047425198892459)
XLA Ops:
  7.3 2.2 copy.27
  9.5 2.0 copy.28
  11.4 7.4 %all-to-all-start.1 = ((bf16[4,64,32,128]{3,2,0,1:T(8,128)(2,1)}), bf16[4,64,32,128]{3,2,0,1:T(8,128)(2,1)}, u32[]{:S(2)}, u32[]{:S(2)}) async-start(bf16[4,64,32,128]{3,2,0,1:T(8,128)(2,1)} %copy.28), calls=%async_computation.1 | async-start | bytes 4194304 | tf_op jit(solution)/shard_map/all_to_all | solution.py:78
  18.9 2.4 copy.23
  21.3 2.0 copy.24
  23.3 49.5 %all-to-all-done.1 = bf16[4,64,32,128]{3,2,0,1:T(8,128)(2,1)} async-done(((bf16[4,64,32,128]{3,2,0,1:T(8,128)(2,1)}), bf16[4,64,32,128]{3,2,0,1:T(8,128)(2,1)}, u32[]{:S(2)}, u32[]{:S(2)}) %all-to-all-start.1) | async-done | bytes 2097184 | tf_op jit(solution)/shard_map/all_to_all | solution.py:78
  72.8 33.3 %all-to-all-start = ((bf16[3,64,56,128]{3,2,0,1:T(8,128)(2,1)}), bf16[3,64,56,128]{3,2,0,1:T(8,128)(2,1)}, u32[]{:S(2)}, u32[]{:S(2)}) async-start(bf16[3,64,56,128]{3,2,0,1:T(8,128)(2,1)} %copy.24), calls=%async_computation | async-start | bytes 5505024 | tf_op jit(solution)/shard_map/all_to_all | solution.py:77
  107.1 3.4 copy.30
  110.6 72.9 %all-to-all-done = bf16[3,64,56,128]{3,2,0,1:T(8,128)(2,1)} async-done(((bf16[3,64,56,128]{3,2,0,1:T(8,128)(2,1)}), bf16[3,64,56,128]{3,2,0,1:T(8,128)(2,1)}, u32[]{:S(2)}, u32[]{:S(2)}) %all-to-all-start) | async-done | bytes 2752544 | tf_op jit(solution)/shard_map/all_to_all | solution.py:77
  183.5 4.0 copy.26
  187.4 113.6 %while.23 = (s32[]{:T(128)}, bf16[4,2,896,128]{3,1,0,2:T(2,128)(2,1)}, s32[4]{0:T(128)S(1)}, bf16[3,4,896,128]{3,2,1,0:T(8,128)(2,1)}, pred[2,4,512]{2,1,0:T(4,1...) while((s32[]{:T(128)}, ...), condition=%wide.region_9.10_spmd, body=%wide.region_0.9_spmd.sunk | while | flops 447742848 | bytes 26686016 | solution.py:116
  190.0 1.8 constant_dynamic-slice_fusion.10
  191.8 2.0 dynamic-slice_bitcast_fusion.3
  193.9 19.6 %while.24 = (s32[]{:T(128)}, bf16[2,2,448,128]{3,2,1,0:T(8,128)(2,1)}, bf16[2,448,128]{2,1,0:T(8,128)(2,1)S(1)}, bf16[896,128]{1,0:T(8,128)(2,1)}, pred[1,1,512]...) while((s32[]{:T(128)}, ...), condition=%wide.region_8.8_spmd, body=%wide.region_1.7_spmd.sunk | while | flops 447742848 | bytes 22390328 | solution.py:113
  193.9 1.4 multiply_reduce_fusion.6
  195.9 2.1 fusion.139
  198.6 1.1 fusion.138
  203.7 1.4 multiply_reduce_fusion.6
  205.7 2.1 fusion.139
  208.4 1.1 fusion.138
  214.6 1.3 copy_dynamic-update-slice_fusion.2
  218.4 1.8 constant_dynamic-slice_fusion.10
  220.3 2.0 dynamic-slice_bitcast_fusion.3
  222.3 19.6 %while.24 = (s32[]{:T(128)}, bf16[2,2,448,128]{3,2,1,0:T(8,128)(2,1)}, bf16[2,448,128]{2,1,0:T(8,128)(2,1)S(1)}, bf16[896,128]{1,0:T(8,128)(2,1)}, pred[1,1,512]...) while((s32[]{:T(128)}, ...), condition=%wide.region_8.8_spmd, body=%wide.region_1.7_spmd.sunk | while | flops 447742848 | bytes 22390328 | solution.py:113
  222.3 1.4 multiply_reduce_fusion.6
  224.3 2.1 fusion.139
  227.0 1.1 fusion.138
  232.1 1.4 multiply_reduce_fusion.6
  234.1 2.1 fusion.139
  236.8 1.1 fusion.138
  243.0 1.3 copy_dynamic-update-slice_fusion.2
  246.8 1.8 constant_dynamic-slice_fusion.10
  248.7 2.0 dynamic-slice_bitcast_fusion.3
  250.7 19.6 %while.24 = (s32[]{:T(128)}, bf16[2,2,448,128]{3,2,1,0:T(8,128)(2,1)}, bf16[2,448,128]{2,1,0:T(8,128)(2,1)S(1)}, bf16[896,128]{1,0:T(8,128)(2,1)}, pred[1,1,512]...) while((s32[]{:T(128)}, ...), condition=%wide.region_8.8_spmd, body=%wide.region_1.7_spmd.sunk | while | flops 447742848 | bytes 22390328 | solution.py:113
  250.7 1.4 multiply_reduce_fusion.6
  252.7 2.1 fusion.139
  255.5 1.1 fusion.138
  260.5 1.4 multiply_reduce_fusion.6
  262.6 2.1 fusion.139
  265.3 1.1 fusion.138
  271.4 1.3 copy_dynamic-update-slice_fusion.2
  275.2 1.8 constant_dynamic-slice_fusion.10
  277.1 2.0 dynamic-slice_bitcast_fusion.3
  279.1 19.6 %while.24 = (s32[]{:T(128)}, bf16[2,2,448,128]{3,2,1,0:T(8,128)(2,1)}, bf16[2,448,128]{2,1,0:T(8,128)(2,1)S(1)}, bf16[896,128]{1,0:T(8,128)(2,1)}, pred[1,1,512]...) while((s32[]{:T(128)}, ...), condition=%wide.region_8.8_spmd, body=%wide.region_1.7_spmd.sunk | while | flops 447742848 | bytes 22390328 | solution.py:113
  279.1 1.4 multiply_reduce_fusion.6
  281.1 2.1 fusion.139
  283.9 1.1 fusion.138
  288.9 1.4 multiply_reduce_fusion.6
  291.0 2.1 fusion.139
  293.7 1.1 fusion.138
  299.8 1.3 copy_dynamic-update-slice_fusion.2
  301.1 27.2 %all-to-all-start.2 = ((bf16[2,4,896,128]{3,0,1,2:T(2,128)(2,1)}), bf16[2,4,896,128]{3,0,1,2:T(2,128)(2,1)}, u32[]{:S(2)}, u32[]{:S(2)}) async-start(bf16[2,4,896,128]{3,0,1,2:T(2,128)(2,1)} %bitcast.168), calls=%async_computation.2 | async-start | bytes 3670016 | tf_op jit(solution)/shard_map/all_to_all | solution.py:119
  329.4 35.5 %all-to-all-done.2 = bf16[2,4,896,128]{3,0,1,2:T(2,128)(2,1)} async-done(((bf16[2,4,896,128]{3,0,1,2:T(2,128)(2,1)}), bf16[2,4,896,128]{3,0,1,2:T(2,128)(2,1)}, u32[]{:S(2)}, u32[]{:S(2)}) %all-to-all-start.2) | async-done | bytes 1835040 | tf_op jit(solution)/shard_map/all_to_all | solution.py:119
  364.9 2.7 copy.44
  367.5 1.3 fusion.105
  368.8 1.3 dot_general.66
  370.1 2.2 dot_general.69
  372.4 4.9 multiply_reduce_fusion.4
  377.3 5.0 multiply_reduce_fusion.3
  382.7 2.8 multiply_reduce_fusion.2
  386.4 3.4 multiply_reduce_fusion.1
  389.8 1.8 fusion.65
  391.6 6.4 %fusion.70 = f32[2048,1536]{1,0:T(8,128)} fusion(bf16[224,1536]{1,0:T(8,128)(2,1)S(1)} %bitcast.167, bf16[28,8,16,128]{3,2,1,0:T(8,128)(2,1)S(1)} %bitcast.164), kind=kOutput, calls=%fused_computation.90 | convolution fusion | flops 1409286144 | bytes 14188544 | tf_op jit(solution)/shard_map/dot_general | solution.py:153
  398.0 140.3 %reduce-scatter.2.cloned.1.call-done = f32[128,1536]{1,0:T(8,128)} async-done(((f32[2048,1536]{1,0:T(8,128)}), f32[128,1536]{1,0:T(8,128)}) %reduce-scatter.2.cloned.1.call-update) | async-done | bytes 786448 | tf_op jit(solution)/shard_map/reduce_scatter | solution.py:152
  (265 shorter events, 51.0 us)
Async XLA Ops:
  6.5 322.1 %copy-start = (bf16[256,3072]{1,0:T(8,128)(2,1)S(1)}, bf16[256,3072]{1,0:T(8,128)(2,1)}, u32[]{:S(2)}) copy-start(bf16[256,3072]{1,0:T(8,128)(2,1)} %param.20) | copy-start | bytes 4718596
  6.5 365.8 %all-gather.3.cloned.1.call-start = ((), (), s32[]{:S(2)}) async-start(), calls=%async_computation.4 | async-start | bytes 6684672 | tf_op jit(solution)/shard_map/all_gather | solution.py:130
  11.4 61.4 %all-to-all-start.1 = ((bf16[4,64,32,128]{3,2,0,1:T(8,128)(2,1)}), bf16[4,64,32,128]{3,2,0,1:T(8,128)(2,1)}, u32[]{:S(2)}, u32[]{:S(2)}) async-start(bf16[4,64,32,128]{3,2,0,1:T(8,128)(2,1)} %copy.28), calls=%async_computation.1 | async-start | bytes 4194304 | tf_op jit(solution)/shard_map/all_to_all | solution.py:78
  23.3 83.6 %copy-start.15 = (s32[2,4,512]{2,1,0:T(4,128)S(1)}, s32[2,4,512]{2,1,0:T(4,128)}, u32[]{:S(2)}) copy-start(s32[2,4,512]{2,1,0:T(4,128)} %param.15) | copy-start | bytes 49156
  72.8 110.7 %all-to-all-start = ((bf16[3,64,56,128]{3,2,0,1:T(8,128)(2,1)}), bf16[3,64,56,128]{3,2,0,1:T(8,128)(2,1)}, u32[]{:S(2)}, u32[]{:S(2)}) async-start(bf16[3,64,56,128]{3,2,0,1:T(8,128)(2,1)} %copy.24), calls=%async_computation | async-start | bytes 5505024 | tf_op jit(solution)/shard_map/all_to_all | solution.py:77
  106.1 271.1 %all-gather.5.cloned.1.call-start = ((), (), s32[]{:S(2)}) async-start(), calls=%async_computation.5 | async-start | bytes 6684672 | tf_op jit(solution)/shard_map/all_gather | solution.py:129
  187.4 2.5 copy-start.17
  187.4 6.4 %copy-start.11 = (pred[2,4,512]{2,1,0:T(4,128)(4,1)}, pred[2,4,512]{2,1,0:T(4,128)(4,1)S(1)}, u32[]{:S(2)}) copy-start(pred[2,4,512]{2,1,0:T(4,128)(4,1)S(1)} %get-tuple-element.467) | copy-start | bytes 12292 | tf_op jit(solution)/shard_map/while
  198.6 1.2 copy-start.1
  199.8 1.2 copy-start.2
  200.9 0.9 copy-start.8
  201.0 1.2 copy-start.7
  201.8 1.0 copy-start.3
  208.4 1.2 copy-start.1
  209.6 1.2 copy-start.2
  210.8 1.2 copy-start.7
  211.7 1.0 copy-start.3
  213.5 2.4 copy-start.12
  213.5 2.4 copy-start.18
  215.9 2.5 copy-start.17
  215.9 6.4 %copy-start.11 = (pred[2,4,512]{2,1,0:T(4,128)(4,1)}, pred[2,4,512]{2,1,0:T(4,128)(4,1)S(1)}, u32[]{:S(2)}) copy-start(pred[2,4,512]{2,1,0:T(4,128)(4,1)S(1)} %get-tuple-element.467) | copy-start | bytes 12292 | tf_op jit(solution)/shard_map/while
  227.0 1.2 copy-start.1
  228.2 1.2 copy-start.2
  229.4 1.2 copy-start.7
  230.3 1.0 copy-start.3
  236.8 1.2 copy-start.1
  238.0 1.2 copy-start.2
  239.2 1.2 copy-start.7
  240.1 1.0 copy-start.3
  241.9 2.4 copy-start.12
  241.9 2.4 copy-start.18
  244.3 2.5 copy-start.17
  244.3 6.4 %copy-start.11 = (pred[2,4,512]{2,1,0:T(4,128)(4,1)}, pred[2,4,512]{2,1,0:T(4,128)(4,1)S(1)}, u32[]{:S(2)}) copy-start(pred[2,4,512]{2,1,0:T(4,128)(4,1)S(1)} %get-tuple-element.467) | copy-start | bytes 12292 | tf_op jit(solution)/shard_map/while
  255.5 1.2 copy-start.1
  256.6 1.2 copy-start.2
  257.8 1.2 copy-start.7
  258.7 1.0 copy-start.3
  265.3 1.2 copy-start.1
  266.4 1.2 copy-start.2
  267.6 1.2 copy-start.7
  268.5 1.0 copy-start.3
  270.3 2.4 copy-start.12
  270.3 2.4 copy-start.18
  272.7 2.5 copy-start.17
  272.7 6.4 %copy-start.11 = (pred[2,4,512]{2,1,0:T(4,128)(4,1)}, pred[2,4,512]{2,1,0:T(4,128)(4,1)S(1)}, u32[]{:S(2)}) copy-start(pred[2,4,512]{2,1,0:T(4,128)(4,1)S(1)} %get-tuple-element.467) | copy-start | bytes 12292 | tf_op jit(solution)/shard_map/while
  283.9 1.2 copy-start.1
  285.0 1.2 copy-start.2
  286.2 1.2 copy-start.7
  287.1 1.0 copy-start.3
  293.7 1.2 copy-start.1
  294.9 1.2 copy-start.2
  296.0 1.2 copy-start.7
  296.9 1.0 copy-start.3
  298.7 2.4 copy-start.12
  298.7 2.4 copy-start.18
  301.1 27.4 %copy-start.16 = (s32[4]{0:T(128)S(1)}, s32[4]{0:T(128)}, u32[]{:S(2)}) copy-start(s32[4]{0:T(128)} %param.16) | copy-start | bytes 52
  301.1 63.8 %all-to-all-start.2 = ((bf16[2,4,896,128]{3,0,1,2:T(2,128)(2,1)}), bf16[2,4,896,128]{3,0,1,2:T(2,128)(2,1)}, u32[]{:S(2)}, u32[]{:S(2)}) async-start(bf16[2,4,896,128]{3,0,1,2:T(2,128)(2,1)} %bitcast.168), calls=%async_computation.2 | async-start | bytes 3670016 | tf_op jit(solution)/shard_map/all_to_all | solution.py:119
  328.2 210.1 %reduce-scatter.2.cloned.1.call-start = ((), (), s32[]{:S(2)}) async-start(), calls=%async_computation.6 | async-start | bytes 13369344 | tf_op jit(solution)/shard_map/reduce_scatter | solution.py:152
  368.8 3.6 copy-start.5
  377.3 5.1 copy-start.10
  377.3 5.3 copy-start.13
  377.3 5.4 copy-start.14
  382.7 2.9 copy-start.9
  389.8 1.8 copy-start.6
  (15 other events, 12.5 us)
Sparse Core Ops, SparseCore 0:
  9.6 98.0 all-gather.2
  110.0 94.7 all-gather.4
  398.2 140.1 reduce-scatter.1
where the time goes:
time: 547 us; the launch traced here: 545 us
  waiting for transfers between devices  300 us (55%)
  matrix products  71 us (13%)
  starting transfers between devices  68.2 us (12%)
  local copies, waits for them, and re-layouts  63.1 us (12%)
  other arithmetic  20.9 us (4%)
  between operations  13.3 us (2%)
  loops' own time  8.68 us (2%)
    reduce_scatter x1, waiting for transfers between devices, shards(): lax.psum_scatter(lax.dot_general(columns, cotangent_rows, (((0,), (0,)),...  140 us
    all_to_all x1, waiting for transfers between devices, shards(): lax.all_to_all(image_local, 'seq', split_axis=1, concat_axis=2, tiled=True)  72.9 us
    all_to_all x1, waiting for transfers between devices, shards(): lax.all_to_all(text_local, 'seq', split_axis=1, concat_axis=2, tiled=True)  49.5 us
    all_to_all x1, waiting for transfers between devices, shards(): lax.all_to_all(both_passes, 'seq', split_axis=2, concat_axis=1, tiled=True)  35.5 us
    all_to_all x1, starting transfers between devices, shards(): lax.all_to_all(image_local, 'seq', split_axis=1, concat_axis=2, tiled=True)  33.3 us
    all_to_all x1, starting transfers between devices, shards(): lax.all_to_all(both_passes, 'seq', split_axis=2, concat_axis=1, tiled=True)  27.2 us
    dot_general x16, matrix products, text_finish(): jnp.dot(queries, text_keys.T, preferred_element_type=jnp.float32) * factor  25.9 us
    while x128, local copies, waits for them, and re-layouts  12.1 us
  transfers between devices with their start and end apart: 6, of which 4 were waited for; matrix products, arithmetic and copies ran while one was open for 22% of the time, Pallas kernels for 0%

commit v1 on v0

--- a/solution.py
+++ b/solution.py
@@ -9,6 +9,18 @@
 HEAD_DIM = 128
 WIDTH = 1536
 TIME_DIM = 256
+
+
+def cut_along(x, dim, count):
+    shape = x.shape
+    blocks = x.reshape(*shape[:dim], count, shape[dim] // count, *shape[dim + 1 :])
+    return jnp.moveaxis(blocks, dim, 0)
+
+
+def laid_out(blocks, dim):
+    lengths = list(blocks.shape[1:])
+    lengths[dim] *= blocks.shape[0]
+    return jnp.moveaxis(blocks, 0, dim).reshape(lengths)
 
 
 def image_block(queries, image_keys, image_values):
@@ -116,7 +128,14 @@
     both_passes = lax.map(joint_item, jnp.arange(owned_count, dtype=jnp.int32)).transpose(
         1, 0, 2, 3
     )
-    returned = lax.all_to_all(both_passes, "seq", split_axis=2, concat_axis=1, tiled=True)
+    size, position_2 = (lax.axis_size("seq"), lax.axis_index("seq"))
+    pieces = cut_along(both_passes, 2, size)
+    outs = [pieces[position_2]]
+    for hop in range(1, size):
+        sent = pieces[position_2 ^ hop]
+        outs.append(lax.ppermute(sent, "seq", [(i, i ^ hop) for i in range(size)]))
+    pieces = jnp.stack(outs)[position_2 ^ jnp.arange(size)]
+    returned = laid_out(pieces, 1)
     attention = returned.reshape(2, HEADS, SAMPLES, image_dev, HEAD_DIM).transpose(0, 2, 3, 1, 4)
     attention = attention.reshape(2, token_rows, HEADS * HEAD_DIM)
     half_dim = TIME_DIM // 2

time: 547 us -> 503 us (0.920)
  matrix products: 71 us -> 43.3 us
  waiting for transfers between devices: 300 us -> 279 us
  starting transfers between devices: 68.2 us -> 82.4 us
    ppermute x0 -> x15, starting transfers between devices: none -> 41.6 us  [shards(): outs.append(lax.ppermute(sent, 'seq', [(i, i ^ hop) for i in range(size)]))]
    all_to_all x1 -> x0, waiting for transfers between devices: 35.5 us -> none  [shards(): lax.all_to_all(both_passes, 'seq', split_axis=2, concat_axis=1, tiled=True)]
    all_to_all x1 -> x0, starting transfers between devices: 27.2 us -> none  [shards(): lax.all_to_all(both_passes, 'seq', split_axis=2, concat_axis=1, tiled=True)]
    dot_general x16, matrix products: 25.9 us -> 6.04 us  [text_finish(): jnp.dot(queries, text_keys.T, preferred_element_type=jnp.float32) * factor]
    ppermute x0 -> x15, waiting for transfers between devices: none -> 14.9 us  [shards(): outs.append(lax.ppermute(sent, 'seq', [(i, i ^ hop) for i in range(size)]))]
    while x128 -> x32, local copies, waits for them, and re-layouts: 12.1 us -> 0.95 us
    unnamed x20 -> x48, local copies, waits for them, and re-layouts: 5 us -> 14.7 us
    another operation x20, other arithmetic: 9.54 us -> 0.38 us
  transfers between devices with their start and end apart: 6 -> 20, of which waited for: 4 -> 8; matrix products, arithmetic and copies ran while one was open for 22% -> 19% of each run, Pallas kernels for 0% -> 0%
where the time goes in v1:
time: 503 us; the launch traced here: 502 us
  waiting for transfers between devices  279 us (55%)
  starting transfers between devices  82.4 us (16%)
  local copies, waits for them, and re-layouts  57.9 us (12%)
  matrix products  43.3 us (9%)
  other arithmetic  17.1 us (3%)
  between operations  13.6 us (3%)
  loops' own time  8.16 us (2%)
    reduce_scatter x1, waiting for transfers between devices, shards(): lax.psum_scatter(lax.dot_general(columns, cotangent_rows, (((0,), (0,)),...  142 us
    all_to_all x1, waiting for transfers between devices, shards(): lax.all_to_all(image_local, 'seq', split_axis=1, concat_axis=2, tiled=True)  71.8 us
    all_to_all x1, waiting for transfers between devices, shards(): lax.all_to_all(text_local, 'seq', split_axis=1, concat_axis=2, tiled=True)  49.5 us
    ppermute x15, starting transfers between devices, shards(): outs.append(lax.ppermute(sent, 'seq', [(i, i ^ hop) for i in range(size)]))  41.6 us
    all_to_all x1, starting transfers between devices, shards(): lax.all_to_all(image_local, 'seq', split_axis=1, concat_axis=2, tiled=True)  33.3 us
    ppermute x15, waiting for transfers between devices, shards(): outs.append(lax.ppermute(sent, 'seq', [(i, i ^ hop) for i in range(size)]))  14.9 us
    unnamed x48, local copies, waits for them, and re-layouts  14.7 us
  transfers between devices with their start and end apart: 20, of which 8 were waited for; matrix products, arithmetic and copies ran while one was open for 19% of the time, Pallas kernels for 0%

profile of v1, /device:TPU:0, one launch (start us, length us, event | category | flops | bytes accessed | tf_op | source)
XLA Modules:
  0.0 501.9 jit_solution(16793743086689737509)
XLA Ops:
  6.5 0.7 all-gather.3.cloned.1.call-update
  7.3 2.2 copy.61
  9.5 2.0 copy.62
  11.4 7.4 %all-to-all-start.1 = ((bf16[4,64,32,128]{3,2,0,1:T(8,128)(2,1)}), bf16[4,64,32,128]{3,2,0,1:T(8,128)(2,1)}, u32[]{:S(2)}, u32[]{:S(2)}) async-start(bf16[4,64,32,128]{3,2,0,1:T(8,128)(2,1)} %copy.62), calls=%async_computation.1 | async-start | bytes 4194304 | tf_op jit(solution)/shard_map/all_to_all | solution.py:90
  18.9 2.4 copy.57
  21.3 2.0 copy.58
  23.3 49.5 %all-to-all-done.1 = bf16[4,64,32,128]{3,2,0,1:T(8,128)(2,1)} async-done(((bf16[4,64,32,128]{3,2,0,1:T(8,128)(2,1)}), bf16[4,64,32,128]{3,2,0,1:T(8,128)(2,1)}, u32[]{:S(2)}, u32[]{:S(2)}) %all-to-all-start.1) | async-done | bytes 2097184 | tf_op jit(solution)/shard_map/all_to_all | solution.py:90
  72.8 33.3 %all-to-all-start = ((bf16[3,64,56,128]{3,2,0,1:T(8,128)(2,1)}), bf16[3,64,56,128]{3,2,0,1:T(8,128)(2,1)}, u32[]{:S(2)}, u32[]{:S(2)}) async-start(bf16[3,64,56,128]{3,2,0,1:T(8,128)(2,1)} %copy.58), calls=%async_computation | async-start | bytes 5505024 | tf_op jit(solution)/shard_map/all_to_all | solution.py:89
  107.5 0.7 fusion.91
  108.2 3.5 copy.64
  111.7 71.8 %all-to-all-done = bf16[3,64,56,128]{3,2,0,1:T(8,128)(2,1)} async-done(((bf16[3,64,56,128]{3,2,0,1:T(8,128)(2,1)}), bf16[3,64,56,128]{3,2,0,1:T(8,128)(2,1)}, u32[]{:S(2)}, u32[]{:S(2)}) %all-to-all-start) | async-done | bytes 2752544 | tf_op jit(solution)/shard_map/all_to_all | solution.py:89
  183.5 4.0 copy.60
  187.4 66.0 %while.23 = (s32[]{:T(128)}, bf16[4,2,896,128]{3,2,1,0:T(8,128)(2,1)}, s32[4]{0:T(128)S(1)}, bf16[3,4,896,128]{3,2,1,0:T(8,128)(2,1)}, pred[2,4,512]{2,1,0:T(4,1...) while((s32[]{:T(128)}, ...), condition=%wide.region_9.10_spmd, body=%wide.region_0.9_spmd.sunk | while | flops 447742848 | bytes 18394864 | solution.py:128
  190.0 1.2 dynamic-slice_bitcast_fusion.3
  191.2 1.8 constant_dynamic-slice_fusion.26
  193.1 9.0 %while.24 = (s32[]{:T(128)}, bf16[2,2,448,128]{3,2,1,0:T(8,128)(2,1)}, bf16[2,448,128]{2,1,0:T(8,128)(2,1)S(1)}, bf16[896,128]{1,0:T(8,128)(2,1)S(1)}, pred[1,1,...) while((s32[]{:T(128)}, ...), condition=%wide.region_8.8_spmd, body=%wide.region_1.7_spmd.sunk | while | flops 447742848 | bytes 14132687 | solution.py:125
  196.9 0.7 fusion.148
  201.4 0.7 fusion.148
  202.1 1.0 copy.141
  203.1 0.8 constant_dynamic-update-slice_fusion.2
  206.5 1.2 dynamic-slice_bitcast_fusion.3
  207.8 1.8 constant_dynamic-slice_fusion.26
  209.6 9.0 %while.24 = (s32[]{:T(128)}, bf16[2,2,448,128]{3,2,1,0:T(8,128)(2,1)}, bf16[2,448,128]{2,1,0:T(8,128)(2,1)S(1)}, bf16[896,128]{1,0:T(8,128)(2,1)S(1)}, pred[1,1,...) while((s32[]{:T(128)}, ...), condition=%wide.region_8.8_spmd, body=%wide.region_1.7_spmd.sunk | while | flops 447742848 | bytes 14132687 | solution.py:125
  213.4 0.7 fusion.148
  217.9 0.7 fusion.148
  218.6 1.0 copy.141
  219.6 0.8 constant_dynamic-update-slice_fusion.2
  223.0 1.2 dynamic-slice_bitcast_fusion.3
  224.2 1.8 constant_dynamic-slice_fusion.26
  226.1 9.0 %while.24 = (s32[]{:T(128)}, bf16[2,2,448,128]{3,2,1,0:T(8,128)(2,1)}, bf16[2,448,128]{2,1,0:T(8,128)(2,1)S(1)}, bf16[896,128]{1,0:T(8,128)(2,1)S(1)}, pred[1,1,...) while((s32[]{:T(128)}, ...), condition=%wide.region_8.8_spmd, body=%wide.region_1.7_spmd.sunk | while | flops 447742848 | bytes 14132687 | solution.py:125
  229.9 0.7 fusion.148
  235.1 1.0 copy.141
  236.1 0.8 constant_dynamic-update-slice_fusion.2
  239.5 1.2 dynamic-slice_bitcast_fusion.3
  240.7 1.8 constant_dynamic-slice_fusion.26
  242.6 9.0 %while.24 = (s32[]{:T(128)}, bf16[2,2,448,128]{3,2,1,0:T(8,128)(2,1)}, bf16[2,448,128]{2,1,0:T(8,128)(2,1)S(1)}, bf16[896,128]{1,0:T(8,128)(2,1)S(1)}, pred[1,1,...) while((s32[]{:T(128)}, ...), condition=%wide.region_8.8_spmd, body=%wide.region_1.7_spmd.sunk | while | flops 447742848 | bytes 14132687 | solution.py:125
  251.6 1.0 copy.141
  252.6 0.8 constant_dynamic-update-slice_fusion.2
  253.4 1.9 constant_dynamic-slice_fusion.7
  255.3 4.1 collective-permute-start
  260.1 12.0 %collective-permute-start.1 = (bf16[2,4,56,128]{3,2,1,0:T(8,128)(2,1)S(1)}, bf16[2,4,56,128]{3,2,1,0:T(8,128)(2,1)S(1)}, u32[]{:S(2)}, u32[]{:S(2)}) collective-permute-start(bf16[2,4,56,128]{3,2,1,0:T(8,128)(2,1)S(1)} %bitcast.260), channel_id=1, source_target_pairs={{0,2},{1,3},{2,0},{3,1},{4,6},{5,7},{6,4},{7,5},{8,10},{9,11},{10,... | collective-permute-start | bytes 344072 | tf_op jit(solution)/shard_map/ppermute | solution.py:136
  272.2 9.9 %collective-permute-start.3 = (bf16[2,4,56,128]{3,2,1,0:T(8,128)(2,1)S(1)}, bf16[2,4,56,128]{3,2,1,0:T(8,128)(2,1)S(1)}, u32[]{:S(2)}, u32[]{:S(2)}) collective-permute-start(bf16[2,4,56,128]{3,2,1,0:T(8,128)(2,1)S(1)} %bitcast.258), channel_id=1, source_target_pairs={{0,4},{1,5},{2,6},{3,7},{4,0},{5,1},{6,2},{7,3},{8,12},{9,13},{10,... | collective-permute-start | bytes 344072 | tf_op jit(solution)/shard_map/ppermute | solution.py:136
  282.4 3.0 collective-permute-start.5
  286.7 2.8 collective-permute-start.7
  290.2 0.9 collective-permute-start.8
  291.7 1.2 collective-permute-start.9
  293.6 1.7 collective-permute-done.5
  295.9 2.0 collective-permute-done.6
  297.9 2.5 collective-permute-start.11
  301.1 0.8 collective-permute-start.12
  302.6 8.5 %collective-permute-done.8 = bf16[2,4,56,128]{3,2,1,0:T(8,128)(2,1)S(1)} collective-permute-done((bf16[2,4,56,128]{3,2,1,0:T(8,128)(2,1)S(1)}, bf16[2,4,56,128]{3,2,1,0:T(8,128)(2,1)S(1)}, u32[]{:S(2)}, u32[]{:S(2)}) %collective-permute-start.8) | collective-permute-done | bytes 114720 | tf_op jit(solution)/shard_map/ppermute | solution.py:136
  311.1 2.3 collective-permute-start.13
  314.0 1.9 collective-permute-start.14
  319.8 2.2 collective-permute-done.14
  322.6 2.4 gather_fusion
  325.5 1.3 dot_general.66
  327.2 1.4 dot_general.69
  328.6 4.6 multiply_reduce_fusion.4
  333.3 5.0 %multiply_reduce_fusion.3 = (f32[4,56]{1,0:T(4,128)S(1)}, f32[4,56,1536]{2,1,0:T(8,128)S(1)}) fusion(bf16[4,56,2048]{2,1,0:T(8,128)(2,1)} %dot_general.69, bf16[2048,1536]{1,0:T(8,128)(2,1)} %all-gather.5.cloned.1.call-done, f32[4,1536]{1,0:T(4,128)S(1)} %get-tuple-element.232, bf16[4,56,1536]{2,1,0:T(8,128)(2,1)} %param.17), kind=kOutput, calls=%fused_computation.81 | convolution fusion | flops 1411006208 | bytes 9298816 | tf_op jit(solution)/shard_map/dot_general | solution.py:153
  338.5 2.7 multiply_reduce_fusion.2
  342.1 3.4 multiply_reduce_fusion.1
  345.5 1.7 fusion.65
  347.2 6.4 %fusion.70 = f32[2048,1536]{1,0:T(8,128)} fusion(bf16[224,1536]{1,0:T(8,128)(2,1)S(1)} %bitcast.245, bf16[28,8,16,128]{3,2,1,0:T(8,128)(2,1)S(1)} %bitcast.242), kind=kOutput, calls=%fused_computation.90 | convolution fusion | flops 1409286144 | bytes 14188544 | tf_op jit(solution)/shard_map/dot_general | solution.py:172
  353.6 141.8 %reduce-scatter.2.cloned.1.call-done = f32[128,1536]{1,0:T(8,128)} async-done(((f32[2048,1536]{1,0:T(8,128)}), f32[128,1536]{1,0:T(8,128)}) %reduce-scatter.2.cloned.1.call-update) | async-done | bytes 786448 | tf_op jit(solution)/shard_map/reduce_scatter | solution.py:171
  (231 shorter events, 49.0 us)
Async XLA Ops:
  6.5 101.0 %copy-start = (bf16[256,3072]{1,0:T(8,128)(2,1)S(1)}, bf16[256,3072]{1,0:T(8,128)(2,1)}, u32[]{:S(2)}) copy-start(bf16[256,3072]{1,0:T(8,128)(2,1)} %param.20) | copy-start | bytes 4718596
  6.5 322.1 %all-gather.3.cloned.1.call-start = ((), (), s32[]{:S(2)}) async-start(), calls=%async_computation.3 | async-start | bytes 6684672 | tf_op jit(solution)/shard_map/all_gather | solution.py:149
  11.4 61.4 %all-to-all-start.1 = ((bf16[4,64,32,128]{3,2,0,1:T(8,128)(2,1)}), bf16[4,64,32,128]{3,2,0,1:T(8,128)(2,1)}, u32[]{:S(2)}, u32[]{:S(2)}) async-start(bf16[4,64,32,128]{3,2,0,1:T(8,128)(2,1)} %copy.62), calls=%async_computation.1 | async-start | bytes 4194304 | tf_op jit(solution)/shard_map/all_to_all | solution.py:90
  23.3 83.7 %copy-start.9 = (s32[4]{0:T(128)S(1)}, s32[4]{0:T(128)}, u32[]{:S(2)}) copy-start(s32[4]{0:T(128)} %param.16) | copy-start | bytes 52
  23.3 84.0 %copy-start.8 = (s32[2,4,512]{2,1,0:T(4,128)S(1)}, s32[2,4,512]{2,1,0:T(4,128)}, u32[]{:S(2)}) copy-start(s32[2,4,512]{2,1,0:T(4,128)} %param.15) | copy-start | bytes 49156
  72.8 110.7 %all-to-all-start = ((bf16[3,64,56,128]{3,2,0,1:T(8,128)(2,1)}), bf16[3,64,56,128]{3,2,0,1:T(8,128)(2,1)}, u32[]{:S(2)}, u32[]{:S(2)}) async-start(bf16[3,64,56,128]{3,2,0,1:T(8,128)(2,1)} %copy.58), calls=%async_computation | async-start | bytes 5505024 | tf_op jit(solution)/shard_map/all_to_all | solution.py:89
  106.2 227.2 %all-gather.5.cloned.1.call-start = ((), (), s32[]{:S(2)}) async-start(), calls=%async_computation.4 | async-start | bytes 6684672 | tf_op jit(solution)/shard_map/all_gather | solution.py:148
  106.9 388.5 %reduce-scatter.2.cloned.1.call-start = ((), (), s32[]{:S(2)}) async-start(), calls=%async_computation.5 | async-start | bytes 13369344 | tf_op jit(solution)/shard_map/reduce_scatter | solution.py:171
  194.9 1.2 copy-start.2
  195.6 0.9 copy-start.3
  199.4 1.2 copy-start.2
  200.1 0.9 copy-start.3
  211.4 1.2 copy-start.2
  212.1 0.9 copy-start.3
  215.9 1.2 copy-start.2
  216.6 0.9 copy-start.3
  227.9 1.2 copy-start.2
  228.6 0.9 copy-start.3
  232.4 1.2 copy-start.2
  233.1 0.9 copy-start.3
  244.4 1.2 copy-start.2
  245.1 0.9 copy-start.3
  248.9 1.2 copy-start.2
  249.6 0.9 copy-start.3
  255.3 27.1 %collective-permute-start = (bf16[2,4,56,128]{3,2,1,0:T(8,128)(2,1)S(1)}, bf16[2,4,56,128]{3,2,1,0:T(8,128)(2,1)S(1)}, u32[]{:S(2)}, u32[]{:S(2)}) collective-permute-start(bf16[2,4,56,128]{3,2,1,0:T(8,128)(2,1)S(1)} %bitcast.261), channel_id=1, source_target_pairs={{0,1},{1,0},{2,3},{3,2},{4,5},{5,4},{6,7},{7,6},{8,9},{9,8},{10,11... | collective-permute-start | bytes 344072 | tf_op jit(solution)/shard_map/ppermute | solution.py:136
  260.1 25.9 %collective-permute-start.1 = (bf16[2,4,56,128]{3,2,1,0:T(8,128)(2,1)S(1)}, bf16[2,4,56,128]{3,2,1,0:T(8,128)(2,1)S(1)}, u32[]{:S(2)}, u32[]{:S(2)}) collective-permute-start(bf16[2,4,56,128]{3,2,1,0:T(8,128)(2,1)S(1)} %bitcast.260), channel_id=1, source_target_pairs={{0,2},{1,3},{2,0},{3,1},{4,6},{5,7},{6,4},{7,5},{8,10},{9,11},{10,... | collective-permute-start | bytes 344072 | tf_op jit(solution)/shard_map/ppermute | solution.py:136
  272.1 14.6 %collective-permute-start.2 = (bf16[2,4,56,128]{3,2,1,0:T(8,128)(2,1)S(1)}, bf16[2,4,56,128]{3,2,1,0:T(8,128)(2,1)S(1)}, u32[]{:S(2)}, u32[]{:S(2)}) collective-permute-start(bf16[2,4,56,128]{3,2,1,0:T(8,128)(2,1)S(1)} %bitcast.259), channel_id=1, source_target_pairs={{0,3},{1,2},{2,1},{3,0},{4,7},{5,6},{6,5},{7,4},{8,11},{9,10},{10,... | collective-permute-start | bytes 344072 | tf_op jit(solution)/shard_map/ppermute | solution.py:136
  272.2 18.0 %collective-permute-start.3 = (bf16[2,4,56,128]{3,2,1,0:T(8,128)(2,1)S(1)}, bf16[2,4,56,128]{3,2,1,0:T(8,128)(2,1)S(1)}, u32[]{:S(2)}, u32[]{:S(2)}) collective-permute-start(bf16[2,4,56,128]{3,2,1,0:T(8,128)(2,1)S(1)} %bitcast.258), channel_id=1, source_target_pairs={{0,4},{1,5},{2,6},{3,7},{4,0},{5,1},{6,2},{7,3},{8,12},{9,13},{10,... | collective-permute-start | bytes 344072 | tf_op jit(solution)/shard_map/ppermute | solution.py:136
  282.2 9.6 %collective-permute-start.4 = (bf16[2,4,56,128]{3,2,1,0:T(8,128)(2,1)S(1)}, bf16[2,4,56,128]{3,2,1,0:T(8,128)(2,1)S(1)}, u32[]{:S(2)}, u32[]{:S(2)}) collective-permute-start(bf16[2,4,56,128]{3,2,1,0:T(8,128)(2,1)S(1)} %bitcast.257), channel_id=1, source_target_pairs={{0,5},{1,4},{2,7},{3,6},{4,1},{5,0},{6,3},{7,2},{8,13},{9,12},{10,... | collective-permute-start | bytes 344072 | tf_op jit(solution)/shard_map/ppermute | solution.py:136
  282.4 12.8 %collective-permute-start.5 = (bf16[2,4,56,128]{3,2,1,0:T(8,128)(2,1)S(1)}, bf16[2,4,56,128]{3,2,1,0:T(8,128)(2,1)S(1)}, u32[]{:S(2)}, u32[]{:S(2)}) collective-permute-start(bf16[2,4,56,128]{3,2,1,0:T(8,128)(2,1)S(1)} %bitcast.256), channel_id=1, source_target_pairs={{0,6},{1,7},{2,4},{3,5},{4,2},{5,3},{6,0},{7,1},{8,14},{9,15},{10,... | collective-permute-start | bytes 344072 | tf_op jit(solution)/shard_map/ppermute | solution.py:136
  286.1 11.9 %collective-permute-start.6 = (bf16[2,4,56,128]{3,2,1,0:T(8,128)(2,1)S(1)}, bf16[2,4,56,128]{3,2,1,0:T(8,128)(2,1)S(1)}, u32[]{:S(2)}, u32[]{:S(2)}) collective-permute-start(bf16[2,4,56,128]{3,2,1,0:T(8,128)(2,1)S(1)} %bitcast.255), channel_id=1, source_target_pairs={{0,7},{1,6},{2,5},{3,4},{4,3},{5,2},{6,1},{7,0},{8,15},{9,14},{10,... | collective-permute-start | bytes 344072 | tf_op jit(solution)/shard_map/ppermute | solution.py:136
  286.7 14.4 %collective-permute-start.7 = (bf16[2,4,56,128]{3,2,1,0:T(8,128)(2,1)S(1)}, bf16[2,4,56,128]{3,2,1,0:T(8,128)(2,1)S(1)}, u32[]{:S(2)}, u32[]{:S(2)}) collective-permute-start(bf16[2,4,56,128]{3,2,1,0:T(8,128)(2,1)S(1)} %bitcast.254), channel_id=1, source_target_pairs={{0,8},{1,9},{2,10},{3,11},{4,12},{5,13},{6,14},{7,15},{8,0},{9,1},... | collective-permute-start | bytes 344072 | tf_op jit(solution)/shard_map/ppermute | solution.py:136
  290.2 20.9 %collective-permute-start.8 = (bf16[2,4,56,128]{3,2,1,0:T(8,128)(2,1)S(1)}, bf16[2,4,56,128]{3,2,1,0:T(8,128)(2,1)S(1)}, u32[]{:S(2)}, u32[]{:S(2)}) collective-permute-start(bf16[2,4,56,128]{3,2,1,0:T(8,128)(2,1)S(1)} %bitcast.253), channel_id=1, source_target_pairs={{0,9},{1,8},{2,11},{3,10},{4,13},{5,12},{6,15},{7,14},{8,1},{9,0},... | collective-permute-start | bytes 344072 | tf_op jit(solution)/shard_map/ppermute | solution.py:136
  291.7 22.3 %collective-permute-start.9 = (bf16[2,4,56,128]{3,2,1,0:T(8,128)(2,1)S(1)}, bf16[2,4,56,128]{3,2,1,0:T(8,128)(2,1)S(1)}, u32[]{:S(2)}, u32[]{:S(2)}) collective-permute-start(bf16[2,4,56,128]{3,2,1,0:T(8,128)(2,1)S(1)} %bitcast.252), channel_id=1, source_target_pairs={{0,10},{1,11},{2,8},{3,9},{4,14},{5,15},{6,12},{7,13},{8,2},{9,3},... | collective-permute-start | bytes 344072 | tf_op jit(solution)/shard_map/ppermute | solution.py:136
  295.3 21.3 %collective-permute-start.10 = (bf16[2,4,56,128]{3,2,1,0:T(8,128)(2,1)S(1)}, bf16[2,4,56,128]{3,2,1,0:T(8,128)(2,1)S(1)}, u32[]{:S(2)}, u32[]{:S(2)}) collective-permute-start(bf16[2,4,56,128]{3,2,1,0:T(8,128)(2,1)S(1)} %bitcast.251), channel_id=1, source_target_pairs={{0,11},{1,10},{2,9},{3,8},{4,15},{5,14},{6,13},{7,12},{8,3},{9,2},... | collective-permute-start | bytes 344072 | tf_op jit(solution)/shard_map/ppermute | solution.py:136
  297.9 19.3 %collective-permute-start.11 = (bf16[2,4,56,128]{3,2,1,0:T(8,128)(2,1)S(1)}, bf16[2,4,56,128]{3,2,1,0:T(8,128)(2,1)S(1)}, u32[]{:S(2)}, u32[]{:S(2)}) collective-permute-start(bf16[2,4,56,128]{3,2,1,0:T(8,128)(2,1)S(1)} %bitcast.250), channel_id=1, source_target_pairs={{0,12},{1,13},{2,14},{3,15},{4,8},{5,9},{6,10},{7,11},{8,4},{9,5},... | collective-permute-start | bytes 344072 | tf_op jit(solution)/shard_map/ppermute | solution.py:136
  301.1 16.8 %collective-permute-start.12 = (bf16[2,4,56,128]{3,2,1,0:T(8,128)(2,1)S(1)}, bf16[2,4,56,128]{3,2,1,0:T(8,128)(2,1)S(1)}, u32[]{:S(2)}, u32[]{:S(2)}) collective-permute-start(bf16[2,4,56,128]{3,2,1,0:T(8,128)(2,1)S(1)} %bitcast.249), channel_id=1, source_target_pairs={{0,13},{1,12},{2,15},{3,14},{4,9},{5,8},{6,11},{7,10},{8,5},{9,4},... | collective-permute-start | bytes 344072 | tf_op jit(solution)/shard_map/ppermute | solution.py:136
  311.1 8.0 %collective-permute-start.13 = (bf16[2,4,56,128]{3,2,1,0:T(8,128)(2,1)S(1)}, bf16[2,4,56,128]{3,2,1,0:T(8,128)(2,1)S(1)}, u32[]{:S(2)}, u32[]{:S(2)}) collective-permute-start(bf16[2,4,56,128]{3,2,1,0:T(8,128)(2,1)S(1)} %bitcast.248), channel_id=1, source_target_pairs={{0,14},{1,15},{2,12},{3,13},{4,10},{5,11},{6,8},{7,9},{8,6},{9,7},... | collective-permute-start | bytes 344072 | tf_op jit(solution)/shard_map/ppermute | solution.py:136
  314.0 7.9 %collective-permute-start.14 = (bf16[2,4,56,128]{3,2,1,0:T(8,128)(2,1)S(1)}, bf16[2,4,56,128]{3,2,1,0:T(8,128)(2,1)S(1)}, u32[]{:S(2)}, u32[]{:S(2)}) collective-permute-start(bf16[2,4,56,128]{3,2,1,0:T(8,128)(2,1)S(1)} %bitcast.247), channel_id=1, source_target_pairs={{0,15},{1,14},{2,13},{3,12},{4,11},{5,10},{6,9},{7,8},{8,7},{9,6},... | collective-permute-start | bytes 344072 | tf_op jit(solution)/shard_map/ppermute | solution.py:136
  327.2 1.4 copy-start.5
  333.3 5.1 %copy-start.6 = (bf16[2048,1536]{1,0:T(8,128)(2,1)S(1)}, bf16[2048,1536]{1,0:T(8,128)(2,1)}, u32[]{:S(2)}) copy-start(bf16[2048,1536]{1,0:T(8,128)(2,1)} %all-gather.5.cloned.1.call-done) | copy-start | bytes 18874372
  333.3 5.2 %copy-start.7 = (bf16[4,56,1536]{2,1,0:T(8,128)(2,1)S(1)}, bf16[4,56,1536]{2,1,0:T(8,128)(2,1)}, u32[]{:S(2)}) copy-start(bf16[4,56,1536]{2,1,0:T(8,128)(2,1)} %param.17) | copy-start | bytes 2064388
  338.5 2.8 copy-start.4
  353.6 141.8 %copy-start.1 = (bf16[256,3072]{1,0:T(8,128)(2,1)S(1)}, bf16[256,3072]{1,0:T(8,128)(2,1)}, u32[]{:S(2)}) copy-start(bf16[256,3072]{1,0:T(8,128)(2,1)} %param.20) | copy-start | bytes 4718596
Sparse Core Ops, SparseCore 0:
  9.6 98.0 all-gather.2
  110.0 94.7 all-gather.4
  353.8 141.6 reduce-scatter.1
